TPU v7x, 32 devices: a whole 2x2x4 slice. The times are simulated.
32 devices in a mesh: pb: 8 (over z, y), ka: 4 (over x, core).
Axes of the slice: x: 2, y: 2, z: 4, core: 2. Of those that a mesh axis runs over, the one named last changes fastest.
Arguments:
- query_rows: bfloat16 [4096, 512], P(('pb', 'ka')), may hold values from -8 to 8
- key_rows: bfloat16 [4096, 128], P(('pb', 'ka')), may hold values from -3 to 3
- value_rows: bfloat16 [4096, 128], P(('pb', 'ka')), may hold values from -6 to 6
- outputs: bfloat16 [4096, 512], P(('pb', 'ka')), may hold values from -3 to 3
- out_grads: bfloat16 [4096, 512], P(('pb', 'ka')), may hold values from -6 to 6
- log_totals: float32 [4, 4096], P(None, ('pb', 'ka'))
- selected: int32 [32, 2], P(('pb', 'ka')), may hold values from 0 to 31, as said below
- counts: int32 [32], P(('pb', 'ka')), may hold values from 1 to 2, as said below
Outputs:
- query_grad: float32 [4096, 512], P(('pb', 'ka'))
- key_grad: float32 [4096, 128], P(('pb', 'ka'))
- value_grad: float32 [4096, 128], P(('pb', 'ka'))
Inputs may be any that keep to these rules, and one draw needn't show every extreme that they name: `selected`: slot 0 of row q is q itself; the first counts[q] entries of row q are distinct blocks no later than q; entries from slot counts[q] on are padding and are ignored. counts[q] is at most q + 1; the last query block's count is 2.
All inputs are finite; a program needn't handle non-finite values.
Results may differ from a plain program's by a relative error of at most 0.0029.
Values may be sent and summed in bfloat16 or wider, within the bound.
A program may use at most 64 MiB of HBM per device.

v0:
```python
import jax
import jax.numpy as jnp
from jax import lax
from jax.sharding import PartitionSpec as P

VERY_LOW = -1e30


def passed_along(value, axis, steps):
    count = lax.axis_size(axis)
    pairs = [(source, (source + steps) % count) for source in range(count)]
    return lax.ppermute(value, axis, pairs)


def head_sums(grad_rows, out_rows, head_width):
    row_total = grad_rows.shape[0]
    part_heads = grad_rows.shape[1] // head_width
    product = grad_rows.astype(jnp.float32) * out_rows.astype(jnp.float32)
    return jnp.sum(product.reshape(row_total, part_heads, head_width), axis=2).T


def shards(query_rows, key_rows, value_rows, outputs, out_grads, log_totals, selected, counts):
    ka_count = lax.axis_size("ka")
    ka_index = lax.axis_index("ka")
    pb_index = lax.axis_index("pb")
    block_count = selected.shape[0]
    slot_count = selected.shape[1]
    head_width = key_rows.shape[1]
    block_rows = query_rows.shape[0] // block_count
    score_scale = head_width ** (-0.5)
    key_pairs = jnp.concatenate([key_rows, value_rows], 1)
    column_keys = lax.all_gather(key_pairs, "pb", axis=0, tiled=True)
    peer_slots, peer_counts = (
        lax.all_gather(selected, "ka", axis=0, tiled=True),
        lax.all_gather(counts, "ka", axis=0, tiled=True),
    )
    key_grads = jnp.zeros((column_keys.shape[0], 2 * head_width), jnp.float32)
    row_offsets = jnp.arange(block_rows, dtype=jnp.int32)
    flat_owner = jnp.repeat(jnp.arange(block_count, dtype=jnp.int32), slot_count)
    flat_slot = jnp.tile(jnp.arange(slot_count, dtype=jnp.int32), block_count)
    flat_places = jnp.arange(block_count * slot_count, dtype=jnp.int32)

    def visit_block(row_stack, query_grad, stat_stack, anchor, key_grads):
        held_query = row_stack[0]
        held_grad = row_stack[1]
        total_rows = stat_stack[0]
        delta_rows = head_sums(row_stack[1], row_stack[2], head_width)
        part_heads = total_rows.shape[0]
        held_slots = lax.dynamic_slice_in_dim(
            peer_slots, anchor * block_count, block_count, 0
        ).reshape(-1)
        held_counts = jnp.repeat(
            lax.dynamic_slice_in_dim(peer_counts, anchor * block_count, block_count, 0), slot_count
        )
        first_block = (pb_index * ka_count + anchor) * block_count
        wanted = (flat_slot < held_counts) & (held_slots // block_count % ka_count == ka_index)
        position = jnp.cumsum(wanted.astype(jnp.int32)) - 1
        placed = wanted[:, None] & (position[:, None] == flat_places[None, :])
        packed_ids = jnp.sum(jnp.where(placed, held_slots[:, None], 0), axis=0)
        packed_owner = jnp.sum(jnp.where(placed, flat_owner[:, None], 0), axis=0)
        live_tiles = jnp.sum(wanted.astype(jnp.int32))

        def one_tile(tile_index, loop_state):
            query_grad, key_grads = loop_state
            key_block = packed_ids[tile_index]
            owner_block = packed_owner[tile_index]
            key_start = (
                key_block // (block_count * ka_count) * block_count + key_block % block_count
            ) * block_rows
            pair_tile = lax.dynamic_slice_in_dim(column_keys, key_start, block_rows, 0)
            key_tile = pair_tile[:, :head_width]
            value_tile = pair_tile[:, head_width:]
            query_tile = held_query.reshape(block_rows, part_heads, head_width)
            grad_tile = held_grad.reshape(block_rows, part_heads, head_width)
            scores = (
                jnp.einsum("rhd,cd->hrc", query_tile, key_tile, preferred_element_type=jnp.float32)
                * score_scale
            )
            query_pos = (first_block + owner_block) * block_rows + row_offsets
            key_pos = key_block * block_rows + row_offsets
            allowed = key_pos[None, :] <= query_pos[:, None]
            probs_full = jnp.exp(
                jnp.where(allowed[None], scores - total_rows[:, :, None], VERY_LOW)
            )
            prob_grads = jnp.einsum(
                "rhd,cd->hrc", grad_tile, value_tile, preferred_element_type=jnp.float32
            )
            score_grads = probs_full * (prob_grads - delta_rows[:, :, None])
            rounded_probs = probs_full.astype(jnp.bfloat16)
            rounded_grads = score_grads.astype(jnp.bfloat16)
            value_part = jnp.einsum(
                "hrc,rhd->cd", rounded_probs, grad_tile, preferred_element_type=jnp.float32
            )
            key_part = (
                jnp.einsum(
                    "hrc,rhd->cd", rounded_grads, query_tile, preferred_element_type=jnp.float32
                )
                * score_scale
            )
            query_part = (
                jnp.einsum(
                    "hrc,cd->rhd", rounded_grads, key_tile, preferred_element_type=jnp.float32
                )
                * score_scale
            )
            old_query = query_grad
            query_grad = old_query + query_part.reshape(block_rows, -1)
            old_keys = lax.dynamic_slice_in_dim(key_grads, key_start, block_rows, 0)
            key_grads = lax.dynamic_update_slice_in_dim(
                key_grads, old_keys + jnp.concatenate([key_part, value_part], 1), key_start, 0
            )
            return (query_grad, key_grads)

        return lax.fori_loop(0, live_tiles, one_tile, (query_grad, key_grads))

    query_part = query_rows
    grad_zero = jnp.zeros(query_part.shape, jnp.float32)
    row_stack = jnp.stack([query_part, out_grads, outputs])
    query_grad = grad_zero
    stat_stack = log_totals[None]

    def forward_hop(hop_index, loop_state):
        row_stack, query_grad, stat_stack, key_grads = loop_state
        anchor = (ka_index - hop_index) % ka_count
        query_grad, key_grads = visit_block(row_stack, query_grad, stat_stack, anchor, key_grads)
        row_stack = passed_along(row_stack, "ka", 1)
        query_grad, stat_stack = passed_along((query_grad, stat_stack), "ka", 1)
        return (row_stack, query_grad, stat_stack, key_grads)

    row_stack, query_grad, stat_stack, key_grads = lax.fori_loop(
        0, ka_count - 1, forward_hop, (row_stack, query_grad, stat_stack, key_grads)
    )
    query_grad, key_grads = visit_block(
        row_stack, query_grad, stat_stack, (ka_index + 1) % ka_count, key_grads
    )
    query_grad = passed_along(query_grad, "ka", 1)
    owned_grads = lax.psum_scatter(key_grads, "pb", scatter_dimension=0, tiled=True)
    return (query_grad, owned_grads[:, :head_width], owned_grads[:, head_width:])


def solution(mesh):
    return jax.shard_map(
        shards,
        mesh=mesh,
        in_specs=(
            P(("pb", "ka"), None),
            P(("pb", "ka"), None),
            P(("pb", "ka"), None),
            P(("pb", "ka"), None),
            P(("pb", "ka"), None),
            P(None, ("pb", "ka")),
            P(("pb", "ka"), None),
            P(("pb", "ka")),
        ),
        out_specs=(P(("pb", "ka"), None), P(("pb", "ka"), None), P(("pb", "ka"), None)),
        check_vma=False,
    )
```

profile of v0, /device:TPU:0, one launch (start us, length us, event | category | flops | bytes accessed | tf_op | source)
XLA Modules:
  0.0 183.4 jit_solution(7212830723820672716)
XLA Ops:
  9.2 0.8 dynamic-update-slice
  10.0 6.4 %all-reduce = s32[4]{0:T(128)S(1)} all-reduce(s32[4]{0:T(128)S(1)} %dynamic-update-slice), channel_id=1, replica_groups=mesh['pb'=8,'ka'=4] {'ka'}, use_global_device_ids=true, to_apply=%add | all-reduce | flops 4 | bytes 32
  17.0 5.0 %all-gather = s32[4,1,2]{2,1,0:T(1,128)S(1)} all-gather(s32[1,1,2]{2,1,0:T(1,128)S(1)} %bitcast.222), channel_id=1, replica_groups=mesh['pb'=8,'ka'=4] {'ka'}, dimensions={0}, use_global_device_ids=true | all-gather | bytes 40 | tf_op jit(solution)/shard_map/all_gather | solution.py:34
  22.7 1.3 convert_reduce_fusion.1
  24.5 1.1 copy.63
  25.7 0.8 copy-done.2
  27.3 31.9 %all_gather.11 = bf16[1024,256]{1,0:T(8,128)(2,1)S(1)} all-gather(bf16[128,256]{1,0:T(8,128)(2,1)S(1)} %pad_maximum_fusion.1), channel_id=1, replica_groups=mesh['pb'=8,'ka'=4] {'pb'}, dimensions={0}, use_global_device_ids=true | all-gather | bytes 589824 | tf_op jit(solution)/shard_map/all_gather | solution.py:32
  60.0 40.6 %while.86 = (s32[]{:T(128)}, bf16[3,128,512]{1,2,0:T(8,128)(2,1)S(1)}, f32[128,512]{0,1:T(8,128)S(1)}, f32[1,4,128]{2,1,0:T(4,128)S(1)}, f32[1024,256]{0,1:T(8,1...) while((s32[]{:T(128)}, ...), condition=%wide.region_7.8_spmd.clone.clone, body=%wide.region_0.7_spmd.clone.clone.sunk | while | flops 84836216 | bytes 8673559 | solution.py:130
  60.7 1.3 convert_reduce_fusion.3
  63.1 6.2 %while.88 = (s32[]{:T(128)}, f32[128,512]{0,1:T(8,128)S(1)}, f32[1024,256]{0,1:T(8,128)S(1)}, s32[]{:T(128)}, s32[2]{0:T(128)S(1)}, /*index=5*/bf16[1024,256]{1,...) while((s32[]{:T(128)}, f32[128,512]{0,1:T(8,128)S(1)}, ...), condition=%wide.region_6.6_spmd.clone, body=%wide.region_5.5_spmd.clone.sunk | while | flops 84574488 | bytes 3415011 | solution.py:114
  69.3 1.0 collective-permute-start.1
  70.3 4.8 %collective-permute-done.1 = f32[128,512]{0,1:T(8,128)S(1)} collective-permute-done((f32[128,512]{0,1:T(8,128)S(1)}, f32[128,512]{0,1:T(8,128)S(1)}, u32[]{:S(2)}, u32[]{:S(2)}) %collective-permute-start.1) | collective-permute-done | bytes 262176 | tf_op jit(solution)/shard_map/while/body/eval_jaxpr/ppermute | solution.py:12
  76.0 1.3 convert_reduce_fusion.3
  78.9 1.0 collective-permute-start.1
  80.0 5.3 %collective-permute-done.1 = f32[128,512]{0,1:T(8,128)S(1)} collective-permute-done((f32[128,512]{0,1:T(8,128)S(1)}, f32[128,512]{0,1:T(8,128)S(1)}, u32[]{:S(2)}, u32[]{:S(2)}) %collective-permute-start.1) | collective-permute-done | bytes 262176 | tf_op jit(solution)/shard_map/while/body/eval_jaxpr/ppermute | solution.py:12
  86.1 1.3 convert_reduce_fusion.3
  88.4 6.2 %while.88 = (s32[]{:T(128)}, f32[128,512]{0,1:T(8,128)S(1)}, f32[1024,256]{0,1:T(8,128)S(1)}, s32[]{:T(128)}, s32[2]{0:T(128)S(1)}, /*index=5*/bf16[1024,256]{1,...) while((s32[]{:T(128)}, f32[128,512]{0,1:T(8,128)S(1)}, ...), condition=%wide.region_6.6_spmd.clone, body=%wide.region_5.5_spmd.clone.sunk | while | flops 84574488 | bytes 3415011 | solution.py:114
  94.7 1.0 collective-permute-start.1
  95.7 4.8 %collective-permute-done.1 = f32[128,512]{0,1:T(8,128)S(1)} collective-permute-done((f32[128,512]{0,1:T(8,128)S(1)}, f32[128,512]{0,1:T(8,128)S(1)}, u32[]{:S(2)}, u32[]{:S(2)}) %collective-permute-start.1) | collective-permute-done | bytes 262176 | tf_op jit(solution)/shard_map/while/body/eval_jaxpr/ppermute | solution.py:12
  100.9 6.4 %while.87 = (s32[]{:T(128)}, f32[128,512]{0,1:T(8,128)S(1)}, f32[1024,256]{0,1:T(8,128)S(1)}, s32[]{:T(128)}, s32[2]{0:T(128)S(1)}, /*index=5*/bf16[1024,256]{1,...) while((s32[]{:T(128)}, f32[128,512]{0,1:T(8,128)S(1)}, ...), condition=%wide.region_13.14_spmd.clone.clone, body=%wide.region_12.13_spmd.clone.clone.sunk | while | flops 84574488 | bytes 3414491 | solution.py:114
  107.4 1.3 copy.67
  108.9 5.8 %collective-permute-done.3 = f32[128,512]{1,0:T(8,128)S(1)} collective-permute-done((f32[128,512]{1,0:T(8,128)S(1)}, f32[128,512]{1,0:T(8,128)S(1)}, u32[]{:S(2)}, u32[]{:S(2)}) %collective-permute-start.3) | collective-permute-done | bytes 262176 | tf_op jit(solution)/shard_map/ppermute | solution.py:12
  114.7 59.6 %reduce-scatter.2.cloned.1.call-done = f32[128,256]{1,0:T(8,128)} async-done(((f32[1024,256]{1,0:T(8,128)}), f32[128,256]{1,0:T(8,128)}) %reduce-scatter.2.cloned.1.call-update) | async-done | bytes 131088 | tf_op jit(solution)/shard_map/reduce_scatter | solution.py:137
  174.3 1.5 fusion.43
  (113 shorter events, 17.3 us)
Async XLA Ops:
  7.2 167.1 %reduce-scatter.2.cloned.1.call-start = ((), (), s32[]{:S(2)}) async-start(), calls=%async_computation.1 | async-start | bytes 1179648 | tf_op jit(solution)/shard_map/reduce_scatter | solution.py:137
  7.9 0.7 copy-start.6
  16.4 0.7 copy-start.5
  24.5 1.1 copy-start.1
  25.6 0.9 copy-start.2
  26.5 0.8 copy-start.3
  26.5 0.8 copy-start.4
  59.3 0.7 copy-start
  60.0 15.2 %collective-permute-start = (bf16[3,128,512]{1,2,0:T(8,128)(2,1)S(1)}, bf16[3,128,512]{1,2,0:T(8,128)(2,1)S(1)}, u32[]{:S(2)}, u32[]{:S(2)}) collective-permute-start(bf16[3,128,512]{1,2,0:T(8,128)(2,1)S(1)} %copy.101), channel_id=1, source_target_pairs={{0,1},{1,2},{2,3},{3,0},{4,5},{5,6},{6,7},{7,4},{8,9},{9,10},{10,1... | collective-permute-start | bytes 1179656 | tf_op jit(solution)/shard_map/while/body/eval_jaxpr/ppermute | solution.py:12
  69.3 5.8 %collective-permute-start.1 = (f32[128,512]{0,1:T(8,128)S(1)}, f32[128,512]{0,1:T(8,128)S(1)}, u32[]{:S(2)}, u32[]{:S(2)}) collective-permute-start(f32[128,512]{0,1:T(8,128)S(1)} %get-tuple-element.1444), channel_id=1, source_target_pairs={{0,1},{1,2},{2,3},{3,0},{4,5},{5,6},{6,7},{7,4},{8,9},{9,10},{10,1... | collective-permute-start | bytes 786440 | tf_op jit(solution)/shard_map/while/body/eval_jaxpr/ppermute | solution.py:12
  70.3 4.9 %collective-permute-start.2 = (f32[1,4,128]{2,1,0:T(4,128)S(1)}, f32[1,4,128]{2,1,0:T(4,128)S(1)}, u32[]{:S(2)}, u32[]{:S(2)}) collective-permute-start(f32[1,4,128]{2,1,0:T(4,128)S(1)} %get-tuple-element.1678), channel_id=1, source_target_pairs={{0,1},{1,2},{2,3},{3,0},{4,5},{5,6},{6,7},{7,4},{8,9},{9,10},{10,1... | collective-permute-start | bytes 6152 | tf_op jit(solution)/shard_map/while/body/eval_jaxpr/ppermute | solution.py:12
  75.2 10.1 %collective-permute-start = (bf16[3,128,512]{1,2,0:T(8,128)(2,1)S(1)}, bf16[3,128,512]{1,2,0:T(8,128)(2,1)S(1)}, u32[]{:S(2)}, u32[]{:S(2)}) collective-permute-start(bf16[3,128,512]{1,2,0:T(8,128)(2,1)S(1)} %copy.101), channel_id=1, source_target_pairs={{0,1},{1,2},{2,3},{3,0},{4,5},{5,6},{6,7},{7,4},{8,9},{9,10},{10,1... | collective-permute-start | bytes 1179656 | tf_op jit(solution)/shard_map/while/body/eval_jaxpr/ppermute | solution.py:12
  78.9 6.3 %collective-permute-start.1 = (f32[128,512]{0,1:T(8,128)S(1)}, f32[128,512]{0,1:T(8,128)S(1)}, u32[]{:S(2)}, u32[]{:S(2)}) collective-permute-start(f32[128,512]{0,1:T(8,128)S(1)} %get-tuple-element.1444), channel_id=1, source_target_pairs={{0,1},{1,2},{2,3},{3,0},{4,5},{5,6},{6,7},{7,4},{8,9},{9,10},{10,1... | collective-permute-start | bytes 786440 | tf_op jit(solution)/shard_map/while/body/eval_jaxpr/ppermute | solution.py:12
  79.9 5.4 %collective-permute-start.2 = (f32[1,4,128]{2,1,0:T(4,128)S(1)}, f32[1,4,128]{2,1,0:T(4,128)S(1)}, u32[]{:S(2)}, u32[]{:S(2)}) collective-permute-start(f32[1,4,128]{2,1,0:T(4,128)S(1)} %get-tuple-element.1678), channel_id=1, source_target_pairs={{0,1},{1,2},{2,3},{3,0},{4,5},{5,6},{6,7},{7,4},{8,9},{9,10},{10,1... | collective-permute-start | bytes 6152 | tf_op jit(solution)/shard_map/while/body/eval_jaxpr/ppermute | solution.py:12
  85.4 15.2 %collective-permute-start = (bf16[3,128,512]{1,2,0:T(8,128)(2,1)S(1)}, bf16[3,128,512]{1,2,0:T(8,128)(2,1)S(1)}, u32[]{:S(2)}, u32[]{:S(2)}) collective-permute-start(bf16[3,128,512]{1,2,0:T(8,128)(2,1)S(1)} %copy.101), channel_id=1, source_target_pairs={{0,1},{1,2},{2,3},{3,0},{4,5},{5,6},{6,7},{7,4},{8,9},{9,10},{10,1... | collective-permute-start | bytes 1179656 | tf_op jit(solution)/shard_map/while/body/eval_jaxpr/ppermute | solution.py:12
  94.7 5.8 %collective-permute-start.1 = (f32[128,512]{0,1:T(8,128)S(1)}, f32[128,512]{0,1:T(8,128)S(1)}, u32[]{:S(2)}, u32[]{:S(2)}) collective-permute-start(f32[128,512]{0,1:T(8,128)S(1)} %get-tuple-element.1444), channel_id=1, source_target_pairs={{0,1},{1,2},{2,3},{3,0},{4,5},{5,6},{6,7},{7,4},{8,9},{9,10},{10,1... | collective-permute-start | bytes 786440 | tf_op jit(solution)/shard_map/while/body/eval_jaxpr/ppermute | solution.py:12
  95.6 4.9 %collective-permute-start.2 = (f32[1,4,128]{2,1,0:T(4,128)S(1)}, f32[1,4,128]{2,1,0:T(4,128)S(1)}, u32[]{:S(2)}, u32[]{:S(2)}) collective-permute-start(f32[1,4,128]{2,1,0:T(4,128)S(1)} %get-tuple-element.1678), channel_id=1, source_target_pairs={{0,1},{1,2},{2,3},{3,0},{4,5},{5,6},{6,7},{7,4},{8,9},{9,10},{10,1... | collective-permute-start | bytes 6152 | tf_op jit(solution)/shard_map/while/body/eval_jaxpr/ppermute | solution.py:12
  108.9 5.8 %collective-permute-start.3 = (f32[128,512]{1,0:T(8,128)S(1)}, f32[128,512]{1,0:T(8,128)S(1)}, u32[]{:S(2)}, u32[]{:S(2)}) collective-permute-start(f32[128,512]{1,0:T(8,128)S(1)} %copy.66), channel_id=1, source_target_pairs={{0,1},{1,2},{2,3},{3,0},{4,5},{5,6},{6,7},{7,4},{8,9},{9,10},{10,1... | collective-permute-start | bytes 786440 | tf_op jit(solution)/shard_map/ppermute | solution.py:12
Sparse Core Ops, SparseCore 0:
  108.9 65.3 reduce-scatter.1
where the time goes:
time: 184 us; the launch traced here: 183 us
  waiting for transfers between devices  80.3 us (44%)
  blocking collectives  43.3 us (24%)
  between operations  14.8 us (8%)
  loops' own time  14.6 us (8%)
  local copies, waits for them, and re-layouts  14.4 us (8%)
  other arithmetic  9.58 us (5%)
  starting transfers between devices  3.4 us (2%)
  matrix products  2.9 us (2%)
    reduce_scatter x1, waiting for transfers between devices, shards(): lax.psum_scatter(key_grads, 'pb', scatter_dimension=0, tiled=True)  59.6 us
    all_gather x1, blocking collectives, shards(): column_keys = lax.all_gather(key_pairs, 'pb', axis=0, tiled=True)  31.9 us
    ppermute x10, waiting for transfers between devices, passed_along(): return lax.ppermute(value, axis, pairs)  20.7 us
    another operation x4, loops' own time, visit_block(): return lax.fori_loop(0, live_tiles, one_tile, (query_grad, key_grads))  14.3 us
    unnamed x21, local copies, waits for them, and re-layouts  6.74 us
    unnamed x1, blocking collectives  6.38 us
    reduce_sum x4, other arithmetic, visit_block(): live_tiles = jnp.sum(wanted.astype(jnp.int32))  5.18 us
    all_gather x1, blocking collectives, shards(): lax.all_gather(selected, 'ka', axis=0, tiled=True)  5.05 us
  transfers between devices with their start and end apart: 11, of which 5 were waited for; matrix products, arithmetic and copies ran while one was open for 7% of the time, Pallas kernels for 0%

commit v1 on v0

--- a/solution.py
+++ b/solution.py
@@ -4,6 +4,26 @@
 from jax.sharding import PartitionSpec as P
 
 VERY_LOW = -1e30
+
+
+def corner_review(array_here, array_dim):
+    array_here = jnp.moveaxis(array_here, 0, array_dim)
+    extra = array_here.shape
+    return array_here.reshape(
+        *extra[:array_dim], extra[array_dim] * extra[array_dim + 1], *extra[array_dim + 2 :]
+    )
+
+
+def _handle_heads(v0, which_axis):
+    wide_n = lax.psum(1, which_axis)
+    heard = v0[None]
+    for s in range(wide_n.bit_length() - 1):
+        back = 1 << s
+        d_next = lax.ppermute(heard, which_axis, [(j0, j0 ^ back) for j0 in range(wide_n)])
+        q_next = jnp.stack([heard, d_next], axis=0)
+        even = lax.axis_index(which_axis) >> s & 1
+        heard = jnp.where(even == 0, q_next, q_next[::-1]).reshape(-1, *v0.shape)
+    return heard
 
 
 def passed_along(value, axis, steps):
@@ -29,7 +49,7 @@
     block_rows = query_rows.shape[0] // block_count
     score_scale = head_width ** (-0.5)
     key_pairs = jnp.concatenate([key_rows, value_rows], 1)
-    column_keys = lax.all_gather(key_pairs, "pb", axis=0, tiled=True)
+    column_keys = corner_review(_handle_heads(key_pairs, "pb"), 0)
     peer_slots, peer_counts = (
         lax.all_gather(selected, "ka", axis=0, tiled=True),
         lax.all_gather(counts, "ka", axis=0, tiled=True),

time: 184 us -> 169 us (0.918)
  blocking collectives: 43.3 us -> 9.95 us
  waiting for transfers between devices: 80.3 us -> 91.3 us
  starting transfers between devices: 3.4 us -> 10.8 us
    all_gather x1 -> x0, blocking collectives: 31.9 us -> none  [shards(): column_keys = lax.all_gather(key_pairs, 'pb', axis=0, tiled=True)]
    ppermute x0 -> x3, waiting for transfers between devices: none -> 12.3 us  [_handle_heads(): lax.ppermute(heard, which_axis, [(j0, j0 ^ back) for j0 in range(wide_n)])]
    ppermute x0 -> x3, starting transfers between devices: none -> 7.36 us  [_handle_heads(): lax.ppermute(heard, which_axis, [(j0, j0 ^ back) for j0 in range(wide_n)])]
    unnamed x21 -> x22, local copies, waits for them, and re-layouts: 6.74 us -> 6.6 us
  transfers between devices with their start and end apart: 11 -> 14, of which waited for: 5 -> 7; matrix products, arithmetic and copies ran while one was open for 7% -> 10% of each run, Pallas kernels for 0% -> 0%
where the time goes in v1:
time: 169 us; the launch traced here: 168 us
  waiting for transfers between devices  91.3 us (54%)
  between operations  14.9 us (9%)
  local copies, waits for them, and re-layouts  14.1 us (8%)
  loops' own time  14 us (8%)
  starting transfers between devices  10.8 us (6%)
  other arithmetic  9.98 us (6%)
  blocking collectives  9.95 us (6%)
  matrix products  2.91 us (2%)
    reduce_scatter x1, waiting for transfers between devices, shards(): lax.psum_scatter(key_grads, 'pb', scatter_dimension=0, tiled=True)  58.2 us
    ppermute x10, waiting for transfers between devices, passed_along(): return lax.ppermute(value, axis, pairs)  20.7 us
    another operation x4, loops' own time, visit_block(): return lax.fori_loop(0, live_tiles, one_tile, (query_grad, key_grads))  13.7 us
    ppermute x3, waiting for transfers between devices, _handle_heads(): lax.ppermute(heard, which_axis, [(j0, j0 ^ back) for j0 in range(wide_n)])  12.3 us
    ppermute x3, starting transfers between devices, _handle_heads(): lax.ppermute(heard, which_axis, [(j0, j0 ^ back) for j0 in range(wide_n)])  7.36 us
    unnamed x22, local copies, waits for them, and re-layouts  6.6 us
    reduce_sum x4, other arithmetic, visit_block(): live_tiles = jnp.sum(wanted.astype(jnp.int32))  5.3 us
    all_gather x1, blocking collectives, shards(): lax.all_gather(selected, 'ka', axis=0, tiled=True)  5.05 us
  transfers between devices with their start and end apart: 14, of which 7 were waited for; matrix products, arithmetic and copies ran while one was open for 10% of the time, Pallas kernels for 0%

profile of v1, /device:TPU:0, one launch (start us, length us, event | category | flops | bytes accessed | tf_op | source)
XLA Modules:
  0.0 167.9 jit_solution(4759237441835660506)
XLA Ops:
  8.0 3.1 %collective-permute-start.3 = (bf16[1,128,256]{2,1,0:T(8,128)(2,1)S(1)}, bf16[1,128,256]{2,1,0:T(8,128)(2,1)S(1)}, u32[]{:S(2)}, u32[]{:S(2)}) collective-permute-start(bf16[1,128,256]{2,1,0:T(8,128)(2,1)S(1)} %bitcast.236), channel_id=1, source_target_pairs={{0,4},{4,0},{8,12},{12,8},{16,20},{20,16},{24,28},{28,24},{1,5},{5... | collective-permute-start | bytes 196616 | tf_op jit(solution)/shard_map/ppermute | solution.py:22
  13.7 4.9 %all-reduce = s32[4]{0:T(128)S(1)} all-reduce(s32[4]{0:T(128)S(1)} %dynamic-update-slice), channel_id=1, replica_groups=mesh['pb'=8,'ka'=4] {'ka'}, use_global_device_ids=true, to_apply=%add | all-reduce | flops 4 | bytes 32
  19.3 5.0 %all-gather = s32[4,1,2]{2,1,0:T(1,128)S(1)} all-gather(s32[1,1,2]{2,1,0:T(1,128)S(1)} %bitcast.242), channel_id=1, replica_groups=mesh['pb'=8,'ka'=4] {'ka'}, dimensions={0}, use_global_device_ids=true | all-gather | bytes 40 | tf_op jit(solution)/shard_map/all_gather | solution.py:54
  25.8 1.6 collective-permute-start.4
  27.5 4.2 %collective-permute-done.4 = bf16[2,128,256]{2,1,0:T(8,128)(2,1)S(1)} collective-permute-done((bf16[2,128,256]{2,1,0:T(8,128)(2,1)S(1)}, bf16[2,128,256]{2,1,0:T(8,128)(2,1)S(1)}, u32[]{:S(2)}, u32[]{:S(2)}) %collective-permute-start.4) | collective-permute-done | bytes 131104 | tf_op jit(solution)/shard_map/ppermute | solution.py:22
  31.7 2.7 %collective-permute-start.5 = (bf16[4,128,256]{2,1,0:T(8,128)(2,1)S(1)}, bf16[4,128,256]{2,1,0:T(8,128)(2,1)S(1)}, u32[]{:S(2)}, u32[]{:S(2)}) collective-permute-start(bf16[4,128,256]{2,1,0:T(8,128)(2,1)S(1)} %bitcast.228), channel_id=1, source_target_pairs={{0,16},{4,20},{8,24},{12,28},{16,0},{20,4},{24,8},{28,12},{1,17},{... | collective-permute-start | bytes 786440 | tf_op jit(solution)/shard_map/ppermute | solution.py:22
  34.4 1.4 convert_reduce_fusion.1
  37.8 8.2 %collective-permute-done.5 = bf16[4,128,256]{2,1,0:T(8,128)(2,1)S(1)} collective-permute-done((bf16[4,128,256]{2,1,0:T(8,128)(2,1)S(1)}, bf16[4,128,256]{2,1,0:T(8,128)(2,1)S(1)}, u32[]{:S(2)}, u32[]{:S(2)}) %collective-permute-start.5) | collective-permute-done | bytes 262176 | tf_op jit(solution)/shard_map/ppermute | solution.py:22
  46.9 39.9 %while.86 = (s32[]{:T(128)}, bf16[3,128,512]{1,2,0:T(8,128)(2,1)S(1)}, f32[128,512]{0,1:T(8,128)S(1)}, f32[1,4,128]{2,1,0:T(4,128)S(1)}, f32[1024,256]{0,1:T(8,1...) while((s32[]{:T(128)}, ...), condition=%wide.region_7.8_spmd.clone.clone, body=%wide.region_0.7_spmd.clone.clone.sunk | while | flops 84836216 | bytes 8673559 | solution.py:150
  47.6 1.3 convert_reduce_fusion.3
  49.9 5.9 %while.88 = (s32[]{:T(128)}, f32[128,512]{0,1:T(8,128)S(1)}, f32[1024,256]{0,1:T(8,128)S(1)}, s32[]{:T(128)}, s32[2]{0:T(128)S(1)}, /*index=5*/bf16[1024,256]{1,...) while((s32[]{:T(128)}, f32[128,512]{0,1:T(8,128)S(1)}, ...), condition=%wide.region_6.6_spmd.clone, body=%wide.region_5.5_spmd.clone.sunk | while | flops 84574488 | bytes 3415011 | solution.py:134
  55.8 1.0 collective-permute-start.1
  56.9 4.8 %collective-permute-done.1 = f32[128,512]{0,1:T(8,128)S(1)} collective-permute-done((f32[128,512]{0,1:T(8,128)S(1)}, f32[128,512]{0,1:T(8,128)S(1)}, u32[]{:S(2)}, u32[]{:S(2)}) %collective-permute-start.1) | collective-permute-done | bytes 262176 | tf_op jit(solution)/shard_map/while/body/eval_jaxpr/ppermute | solution.py:32
  62.5 1.3 convert_reduce_fusion.3
  65.4 1.0 collective-permute-start.1
  66.5 5.3 %collective-permute-done.1 = f32[128,512]{0,1:T(8,128)S(1)} collective-permute-done((f32[128,512]{0,1:T(8,128)S(1)}, f32[128,512]{0,1:T(8,128)S(1)}, u32[]{:S(2)}, u32[]{:S(2)}) %collective-permute-start.1) | collective-permute-done | bytes 262176 | tf_op jit(solution)/shard_map/while/body/eval_jaxpr/ppermute | solution.py:32
  72.6 1.3 convert_reduce_fusion.3
  75.0 5.9 %while.88 = (s32[]{:T(128)}, f32[128,512]{0,1:T(8,128)S(1)}, f32[1024,256]{0,1:T(8,128)S(1)}, s32[]{:T(128)}, s32[2]{0:T(128)S(1)}, /*index=5*/bf16[1024,256]{1,...) while((s32[]{:T(128)}, f32[128,512]{0,1:T(8,128)S(1)}, ...), condition=%wide.region_6.6_spmd.clone, body=%wide.region_5.5_spmd.clone.sunk | while | flops 84574488 | bytes 3415011 | solution.py:134
  81.9 4.8 %collective-permute-done.1 = f32[128,512]{0,1:T(8,128)S(1)} collective-permute-done((f32[128,512]{0,1:T(8,128)S(1)}, f32[128,512]{0,1:T(8,128)S(1)}, u32[]{:S(2)}, u32[]{:S(2)}) %collective-permute-start.1) | collective-permute-done | bytes 262176 | tf_op jit(solution)/shard_map/while/body/eval_jaxpr/ppermute | solution.py:32
  86.9 6.5 %while.87 = (s32[]{:T(128)}, f32[128,512]{0,1:T(8,128)S(1)}, f32[1024,256]{0,1:T(8,128)S(1)}, s32[]{:T(128)}, s32[2]{0:T(128)S(1)}, /*index=5*/bf16[1024,256]{1,...) while((s32[]{:T(128)}, f32[128,512]{0,1:T(8,128)S(1)}, ...), condition=%wide.region_13.14_spmd.clone.clone, body=%wide.region_12.13_spmd.clone.clone.sunk | while | flops 84574488 | bytes 3414491 | solution.py:134
  93.3 1.3 copy.67
  94.9 5.8 %collective-permute-done.6 = f32[128,512]{1,0:T(8,128)S(1)} collective-permute-done((f32[128,512]{1,0:T(8,128)S(1)}, f32[128,512]{1,0:T(8,128)S(1)}, u32[]{:S(2)}, u32[]{:S(2)}) %collective-permute-start.6) | collective-permute-done | bytes 262176 | tf_op jit(solution)/shard_map/ppermute | solution.py:32
  100.7 58.2 %reduce-scatter.2.cloned.1.call-done = f32[128,256]{1,0:T(8,128)} async-done(((f32[1024,256]{1,0:T(8,128)}), f32[128,256]{1,0:T(8,128)}) %reduce-scatter.2.cloned.1.call-update) | async-done | bytes 131088 | tf_op jit(solution)/shard_map/reduce_scatter | solution.py:157
  158.8 1.5 fusion.45
  (125 shorter events, 21.0 us)
Async XLA Ops:
  7.2 151.7 %reduce-scatter.2.cloned.1.call-start = ((), (), s32[]{:S(2)}) async-start(), calls=%async_computation.1 | async-start | bytes 1179648 | tf_op jit(solution)/shard_map/reduce_scatter | solution.py:157
  7.2 0.8 copy-start.4
  8.0 17.8 %collective-permute-start.3 = (bf16[1,128,256]{2,1,0:T(8,128)(2,1)S(1)}, bf16[1,128,256]{2,1,0:T(8,128)(2,1)S(1)}, u32[]{:S(2)}, u32[]{:S(2)}) collective-permute-start(bf16[1,128,256]{2,1,0:T(8,128)(2,1)S(1)} %bitcast.236), channel_id=1, source_target_pairs={{0,4},{4,0},{8,12},{12,8},{16,20},{20,16},{24,28},{28,24},{1,5},{5... | collective-permute-start | bytes 196616 | tf_op jit(solution)/shard_map/ppermute | solution.py:22
  11.7 0.7 copy-start.6
  18.6 0.7 copy-start.5
  25.8 5.8 %collective-permute-start.4 = (bf16[2,128,256]{2,1,0:T(8,128)(2,1)S(1)}, bf16[2,128,256]{2,1,0:T(8,128)(2,1)S(1)}, u32[]{:S(2)}, u32[]{:S(2)}) collective-permute-start(bf16[2,128,256]{2,1,0:T(8,128)(2,1)S(1)} %get-tuple-element.1225), channel_id=1, source_target_pairs={{0,8},{4,12},{8,0},{12,4},{16,24},{20,28},{24,16},{28,20},{1,9},{5... | collective-permute-start | bytes 393224 | tf_op jit(solution)/shard_map/ppermute | solution.py:22
  31.7 4.1 %copy-start.1 = (bf16[128,512]{1,0:T(8,128)(2,1)S(1)}, bf16[128,512]{1,0:T(8,128)(2,1)}, u32[]{:S(2)}) copy-start(bf16[128,512]{1,0:T(8,128)(2,1)} %param.17) | copy-start | bytes 393220
  31.7 14.3 %collective-permute-start.5 = (bf16[4,128,256]{2,1,0:T(8,128)(2,1)S(1)}, bf16[4,128,256]{2,1,0:T(8,128)(2,1)S(1)}, u32[]{:S(2)}, u32[]{:S(2)}) collective-permute-start(bf16[4,128,256]{2,1,0:T(8,128)(2,1)S(1)} %bitcast.228), channel_id=1, source_target_pairs={{0,16},{4,20},{8,24},{12,28},{16,0},{20,4},{24,8},{28,12},{1,17},{... | collective-permute-start | bytes 786440 | tf_op jit(solution)/shard_map/ppermute | solution.py:22
  35.8 0.9 copy-start.2
  36.7 0.9 copy-start.3
  46.2 0.7 copy-start
  46.9 14.8 %collective-permute-start = (bf16[3,128,512]{1,2,0:T(8,128)(2,1)S(1)}, bf16[3,128,512]{1,2,0:T(8,128)(2,1)S(1)}, u32[]{:S(2)}, u32[]{:S(2)}) collective-permute-start(bf16[3,128,512]{1,2,0:T(8,128)(2,1)S(1)} %copy.102), channel_id=1, source_target_pairs={{0,1},{1,2},{2,3},{3,0},{4,5},{5,6},{6,7},{7,4},{8,9},{9,10},{10,1... | collective-permute-start | bytes 1179656 | tf_op jit(solution)/shard_map/while/body/eval_jaxpr/ppermute | solution.py:32
  55.8 5.8 %collective-permute-start.1 = (f32[128,512]{0,1:T(8,128)S(1)}, f32[128,512]{0,1:T(8,128)S(1)}, u32[]{:S(2)}, u32[]{:S(2)}) collective-permute-start(f32[128,512]{0,1:T(8,128)S(1)} %get-tuple-element.1446), channel_id=1, source_target_pairs={{0,1},{1,2},{2,3},{3,0},{4,5},{5,6},{6,7},{7,4},{8,9},{9,10},{10,1... | collective-permute-start | bytes 786440 | tf_op jit(solution)/shard_map/while/body/eval_jaxpr/ppermute | solution.py:32
  56.8 4.9 %collective-permute-start.2 = (f32[1,4,128]{2,1,0:T(4,128)S(1)}, f32[1,4,128]{2,1,0:T(4,128)S(1)}, u32[]{:S(2)}, u32[]{:S(2)}) collective-permute-start(f32[1,4,128]{2,1,0:T(4,128)S(1)} %get-tuple-element.1680), channel_id=1, source_target_pairs={{0,1},{1,2},{2,3},{3,0},{4,5},{5,6},{6,7},{7,4},{8,9},{9,10},{10,1... | collective-permute-start | bytes 6152 | tf_op jit(solution)/shard_map/while/body/eval_jaxpr/ppermute | solution.py:32
  61.8 10.1 %collective-permute-start = (bf16[3,128,512]{1,2,0:T(8,128)(2,1)S(1)}, bf16[3,128,512]{1,2,0:T(8,128)(2,1)S(1)}, u32[]{:S(2)}, u32[]{:S(2)}) collective-permute-start(bf16[3,128,512]{1,2,0:T(8,128)(2,1)S(1)} %copy.102), channel_id=1, source_target_pairs={{0,1},{1,2},{2,3},{3,0},{4,5},{5,6},{6,7},{7,4},{8,9},{9,10},{10,1... | collective-permute-start | bytes 1179656 | tf_op jit(solution)/shard_map/while/body/eval_jaxpr/ppermute | solution.py:32
  65.4 6.4 %collective-permute-start.1 = (f32[128,512]{0,1:T(8,128)S(1)}, f32[128,512]{0,1:T(8,128)S(1)}, u32[]{:S(2)}, u32[]{:S(2)}) collective-permute-start(f32[128,512]{0,1:T(8,128)S(1)} %get-tuple-element.1446), channel_id=1, source_target_pairs={{0,1},{1,2},{2,3},{3,0},{4,5},{5,6},{6,7},{7,4},{8,9},{9,10},{10,1... | collective-permute-start | bytes 786440 | tf_op jit(solution)/shard_map/while/body/eval_jaxpr/ppermute | solution.py:32
  66.4 5.4 %collective-permute-start.2 = (f32[1,4,128]{2,1,0:T(4,128)S(1)}, f32[1,4,128]{2,1,0:T(4,128)S(1)}, u32[]{:S(2)}, u32[]{:S(2)}) collective-permute-start(f32[1,4,128]{2,1,0:T(4,128)S(1)} %get-tuple-element.1680), channel_id=1, source_target_pairs={{0,1},{1,2},{2,3},{3,0},{4,5},{5,6},{6,7},{7,4},{8,9},{9,10},{10,1... | collective-permute-start | bytes 6152 | tf_op jit(solution)/shard_map/while/body/eval_jaxpr/ppermute | solution.py:32
  71.9 14.8 %collective-permute-start = (bf16[3,128,512]{1,2,0:T(8,128)(2,1)S(1)}, bf16[3,128,512]{1,2,0:T(8,128)(2,1)S(1)}, u32[]{:S(2)}, u32[]{:S(2)}) collective-permute-start(bf16[3,128,512]{1,2,0:T(8,128)(2,1)S(1)} %copy.102), channel_id=1, source_target_pairs={{0,1},{1,2},{2,3},{3,0},{4,5},{5,6},{6,7},{7,4},{8,9},{9,10},{10,1... | collective-permute-start | bytes 1179656 | tf_op jit(solution)/shard_map/while/body/eval_jaxpr/ppermute | solution.py:32
  80.9 5.8 %collective-permute-start.1 = (f32[128,512]{0,1:T(8,128)S(1)}, f32[128,512]{0,1:T(8,128)S(1)}, u32[]{:S(2)}, u32[]{:S(2)}) collective-permute-start(f32[128,512]{0,1:T(8,128)S(1)} %get-tuple-element.1446), channel_id=1, source_target_pairs={{0,1},{1,2},{2,3},{3,0},{4,5},{5,6},{6,7},{7,4},{8,9},{9,10},{10,1... | collective-permute-start | bytes 786440 | tf_op jit(solution)/shard_map/while/body/eval_jaxpr/ppermute | solution.py:32
  81.8 4.9 %collective-permute-start.2 = (f32[1,4,128]{2,1,0:T(4,128)S(1)}, f32[1,4,128]{2,1,0:T(4,128)S(1)}, u32[]{:S(2)}, u32[]{:S(2)}) collective-permute-start(f32[1,4,128]{2,1,0:T(4,128)S(1)} %get-tuple-element.1680), channel_id=1, source_target_pairs={{0,1},{1,2},{2,3},{3,0},{4,5},{5,6},{6,7},{7,4},{8,9},{9,10},{10,1... | collective-permute-start | bytes 6152 | tf_op jit(solution)/shard_map/while/body/eval_jaxpr/ppermute | solution.py:32
  94.8 5.8 %collective-permute-start.6 = (f32[128,512]{1,0:T(8,128)S(1)}, f32[128,512]{1,0:T(8,128)S(1)}, u32[]{:S(2)}, u32[]{:S(2)}) collective-permute-start(f32[128,512]{1,0:T(8,128)S(1)} %copy.66), channel_id=1, source_target_pairs={{0,1},{1,2},{2,3},{3,0},{4,5},{5,6},{6,7},{7,4},{8,9},{9,10},{10,1... | collective-permute-start | bytes 786440 | tf_op jit(solution)/shard_map/ppermute | solution.py:32
Sparse Core Ops, SparseCore 0:
  94.8 64.0 reduce-scatter.1
